TPU v7x, 512 devices: a whole 4x4x16 slice. The times are simulated.
512 devices in a mesh: col: 64 (over x, z), tm: 8 (over y, core).
Axes of the slice: x: 4, y: 4, z: 16, core: 2. Of those that a mesh axis runs over, the one named last changes fastest.
Arguments:
- series: bfloat16 [1200, 98304], P(None, 'col'), may hold values from -700 to 700
- slab_series: float32 [1200, 2048], P('tm', 'col'), may hold values from -700 to 700
- phase_index: int32 [4, 600], P(None, 'tm'), may hold values from 0 to 1199
Outputs:
- tile_peak: float32 [4, 2048, 64], P(None, None, 'col')
- peak_all: float32 [4], replicated
All inputs are finite; a program needn't handle non-finite values.
Results may differ from a plain program's by a relative error of at most 0.0013.
Values may be sent and summed in bfloat16 or wider, within the bound.
A program may use at most 64 MiB of HBM per device.

v0:
```python
import functools
import math
import jax
import jax.numpy as jnp
from jax import lax
from jax.sharding import Mesh
from jax.sharding import PartitionSpec as P

FRAMES = 1200
FREQS = 600
COL = ("col_0", "col_1")
EPSILON = 1e-06
HIGHEST = lax.Precision.HIGHEST


def laid_out(parts, dim):
    shape = list(parts.shape[1:])
    shape[dim] *= parts.shape[0]
    return jnp.moveaxis(parts, 0, dim).reshape(shape)


def sent_to_all(value, axis):
    copies = jnp.broadcast_to(value, (lax.axis_size(axis), *value.shape))
    return lax.all_to_all(copies, axis, split_axis=0, concat_axis=0, tiled=True)


def gathered_copies(value, axis, dim):
    return laid_out(sent_to_all(value, axis), dim)


def all_blocks(value, axes, sequence):
    parts = value[None]
    for k in sequence:
        parts = lax.all_gather(parts, axes[k], axis=0, tiled=True)
    current = [lax.axis_size(axes[k]) for k in reversed(sequence)]
    parts = parts.reshape(*current, *value.shape)
    turned = sorted(range(len(sequence)), key=lambda place: sequence[len(sequence) - 1 - place])
    return parts.transpose(*turned, *range(len(sequence), parts.ndim)).reshape(-1, *value.shape)


def gathered_by_axis(value, axes, sequence, dim):
    return laid_out(all_blocks(value, axes, sequence), dim)


def by_axis(value, axes):
    return functools.reduce(lax.pmax, axes, value)


def twiddle(frame_ids, freq_ids):
    turn_count = frame_ids[:, None] * freq_ids[None, :] % FRAMES
    angles = turn_count.astype(jnp.float32) * (2.0 * math.pi / FRAMES)
    return (jnp.cos(angles), jnp.sin(angles))


def rotate_back(spec_cos, spec_sin, phase_ids, freq_ids, cos_back, sin_back):
    phase_angle = phase_ids.astype(jnp.float32) * (2.0 * math.pi / FRAMES)
    phase_cos = jnp.cos(phase_angle)[:, :, None]
    phase_sin = jnp.sin(phase_angle)[:, :, None]
    weights = (jnp.where(freq_ids < FREQS, 2.0, 1.0) / FRAMES).astype(jnp.float32)[None, :, None]
    rot_real = (spec_cos[None] * phase_cos + spec_sin[None] * phase_sin) * weights
    rot_imag = (spec_cos[None] * phase_sin - spec_sin[None] * phase_cos) * weights
    return jnp.einsum("sfv,tf->svt", rot_real, cos_back, precision=HIGHEST) - jnp.einsum(
        "sfv,tf->svt", rot_imag, sin_back, precision=HIGHEST
    )


def normalize_rows(surrogate):
    return (
        surrogate * lax.rsqrt(jnp.sum(surrogate * surrogate, axis=2, keepdims=True) + EPSILON)
    ).astype(jnp.bfloat16)


def peak_update(normed_rows, normed_cols):
    scores = jnp.einsum("srt,tc->src", normed_rows, normed_cols, preferred_element_type=jnp.float32)
    row_top = jnp.max(jnp.abs(scores), axis=2)
    return row_top


def body(series, slab_series, phase_index):
    values = series.astype(jnp.float32)
    centered = values - jnp.mean(values, axis=0, keepdims=True)
    normed_cols = (
        centered * lax.rsqrt(jnp.sum(centered * centered, axis=0, keepdims=True) + EPSILON)
    ).astype(jnp.bfloat16)
    surr_count = phase_index.shape[0]
    n_col = lax.axis_size(COL)
    n_tm = lax.axis_size("tm")
    row_share = slab_series.shape[1] // n_tm
    own_frames = lax.all_to_all(slab_series, "tm", split_axis=1, concat_axis=0, tiled=True)
    own_phase = gathered_copies(phase_index, "tm", 1)
    every_freq = jnp.arange(1, FREQS + 1, dtype=jnp.int32)
    cos_every, sin_every = twiddle(jnp.arange(FRAMES, dtype=jnp.int32), every_freq)
    own_cos = jnp.dot(cos_every.T, own_frames, precision=HIGHEST)
    own_sin = jnp.dot(sin_every.T, own_frames, precision=HIGHEST)
    own_normed = normalize_rows(
        rotate_back(own_cos, own_sin, own_phase, every_freq, cos_every, sin_every)
    )
    running = peak_update(gathered_by_axis(own_normed, COL, (0, 1), 1), normed_cols)
    scaled = running * math.sqrt(FRAMES)
    gathered = gathered_copies(scaled.reshape(surr_count, n_col, 1, row_share), "tm", 2)
    full_peaks = gathered.reshape(surr_count, n_col * n_tm * row_share)
    peak_all = by_axis(jnp.max(full_peaks, axis=1), COL)
    return (full_peaks[:, :, None], peak_all)


def solution(mesh):
    finer = Mesh(mesh.devices.reshape(4, 16, mesh.shape["tm"]), ("col_0", "col_1", "tm"))
    placed = (P(None, COL), P("tm", COL), P(None, "tm"))
    return jax.shard_map(
        body, mesh=finer, in_specs=placed, out_specs=(P(None, None, COL), P()), check_vma=False
    )
```

profile of v0, /device:TPU:8, one launch (start us, length us, event | category | flops | bytes accessed | tf_op | source)
XLA Modules:
  0.0 242.8 jit_solution(10669539949304442477)
XLA Ops:
  7.2 1.3 broadcast_in_dim.14
  8.4 9.0 %all-to-all-start.1 = ((s32[8,4,75]{2,1,0:T(4,128)}), s32[8,4,75]{2,1,0:T(4,128)S(1)}, u32[]{:S(2)}, u32[]{:S(2)}) async-start(s32[8,4,75]{2,1,0:T(4,128)} %broadcast_in_dim.14), calls=%async_computation.1 | async-start | bytes 32768 | tf_op jit(solution)/shard_map/all_to_all | solution.py:24
  17.5 1.4 all_to_all.20
  18.9 2.5 %all-to-all-done.1 = s32[8,4,75]{2,1,0:T(4,128)S(1)} async-done(((s32[8,4,75]{2,1,0:T(4,128)}), s32[8,4,75]{2,1,0:T(4,128)S(1)}, u32[]{:S(2)}, u32[]{:S(2)}) %all-to-all-start.1) | async-done | bytes 9632 | tf_op jit(solution)/shard_map/all_to_all | solution.py:24
  21.4 4.7 %all-to-all-start = ((f32[150,8,4]{0,2,1:T(4,128)}), f32[150,8,4]{0,2,1:T(4,128)S(1)}, u32[]{:S(2)}, u32[]{:S(2)}) async-start(f32[150,8,4]{0,2,1:T(4,128)} %all_to_all.20), calls=%async_computation | async-start | bytes 65536 | tf_op jit(solution)/shard_map/all_to_all | solution.py:89
  26.1 0.1 cosine_bitcast_fusion
  26.4 3.7 %all-to-all-done = f32[150,8,4]{0,2,1:T(4,128)S(1)} async-done(((f32[150,8,4]{0,2,1:T(4,128)}), f32[150,8,4]{0,2,1:T(4,128)S(1)}, u32[]{:S(2)}, u32[]{:S(2)}) %all-to-all-start) | async-done | bytes 19232 | tf_op jit(solution)/shard_map/all_to_all | solution.py:89
  30.1 0.1 all_to_all.23
  30.2 14.0 %fusion.19 = f32[600,4]{0,1:T(4,128)S(1)} fusion(f32[1200,4]{0,1:T(4,128)S(1)} %all_to_all.23, s32[600]{0:T(1024)S(1)} %iota_add_fusion), kind=kOutput, calls=%fused_computation.22 | convolution fusion | flops 41040000 | bytes 31200 | tf_op jit(solution)/shard_map/dot_general | solution.py:93
  44.2 14.1 %fusion.22 = f32[600,4]{0,1:T(4,128)S(1)} fusion(f32[1200,4]{0,1:T(4,128)S(1)} %all_to_all.23, s32[600]{0:T(1024)S(1)} %iota_add_fusion), kind=kOutput, calls=%fused_computation.23 | convolution fusion | flops 41040000 | bytes 31200 | tf_op jit(solution)/shard_map/dot_general | solution.py:94
  58.3 15.3 %fusion.10 = f32[4,4,1200]{2,1,0:T(4,128)S(1)} fusion(s32[600]{0:T(1024)S(1)} %iota_add_fusion, f32[600]{0:T(1024)S(1)} %select_multiply_fusion, f32[4,600]{1,0:T(4,128)S(1)} %sin.21, f32[600,4]{0,1:T(4,128)S(1)} %fusion.22, f32[4,600]{1,0:T(4,128)S(1)} %cos.21, f32[600,4]{0,1:T(4,128)S(1)} %fusion.19), kind=kOutput, calls=%fused_computation.13 | convolution fusion | flops 144758400 | bytes 120000 | tf_op jit(solution)/shard_map/sfv,tf->svt/dot_general | solution.py:62
  73.6 15.3 %multiply_reduce_fusion = (f32[4,4]{1,0:T(4,128)S(1)}, f32[4,4,1200]{2,1,0:T(4,128)S(1)}) fusion(f32[4,4,1200]{2,1,0:T(4,128)S(1)} %fusion.10, s32[600]{0:T(1024)S(1)} %iota_add_fusion, f32[600]{0:T(1024)S(1)} %select_multiply_fusion, f32[4,600]{1,0:T(4,128)S(1)} %sin.21, f32[600,4]{0,1:T(4,128)S(1)} %fusion.22, f32[4,600]{1,0:T(4,128)S(1)} %cos.21, ...), kind=kOutput, calls=%fused_computation.40 | convolution fusion | flops 144815984 | bytes 196864 | tf_op jit(solution)/shard_map/sfv,tf->svt/dot_general | solution.py:62
  88.9 0.1 multiply_convert_fusion
  89.0 13.1 %all-gather = bf16[16,4,1200]{2,1,0:T(4,128)(2,1)} all-gather(bf16[4,4,1200]{2,1,0:T(4,128)(2,1)S(1)} %multiply_convert_fusion), channel_id=2, replica_groups=mesh['col_0'=4,'col_1'=16,'tm'=8] {'col_0'}, dimensions={0}, use_global_device_ids=true | all-gather | bytes 192000 | tf_op jit(solution)/shard_map/all_gather | solution.py:34
  102.1 2.8 %convert_reduce_fusion = f32[1536]{0:T(1024)S(1)} fusion(bf16[1200,1536]{1,0:T(8,128)(2,1)} %param.3), kind=kLoop, calls=%fused_computation.1 | loop fusion | flops 3684864 | bytes 3692544 | tf_op jit(solution)/shard_map/reduce_sum | solution.py:81
  104.9 0.4 copy-done
  105.2 1.0 fusion.2
  106.3 69.0 %all-gather.3.cloned.1.call-done = bf16[64,4,4,1200]{3,2,1,0:T(4,128)(2,1)} async-done(((bf16[4,4,4,1200]{3,2,1,0:T(4,128)(2,1)}), bf16[64,4,4,1200]{3,2,1,0:T(4,128)(2,1)}) %all-gather.3.cloned.1.call-update) | async-done | bytes 2457616 | tf_op jit(solution)/shard_map/all_gather | solution.py:34
  175.3 3.0 %copy.19 = bf16[4,16,4,4,1200]{4,2,3,1,0:T(4,128)(2,1)S(1)} copy(bf16[4,16,4,4,1200]{4,3,2,0,1:T(4,128)(2,1)} %bitcast.44) | data formatting | bytes 4915200 | tf_op jit(solution)/shard_map/transpose | solution.py:38
  178.2 4.7 %abs_reduce_fusion = f32[4,256]{1,0:T(4,128)S(1)} fusion(bf16[1200,1536]{1,0:T(8,128)(2,1)S(1)} %copy-done.1, f32[1536]{0:T(1024)S(1)} %add_rsqrt_fusion, f32[1536]{0:T(1024)S(1)} %broadcast_multiply_fusion, bf16[4,256,1200]{2,0,1:T(4,128)(2,1)S(1)} %bitcast.45), kind=kOutput, calls=%fused_computation.6 | convolution fusion | flops 3785391104 | bytes 6160384 | tf_op jit(solution)/shard_map/srt,tc->src/dot_general | solution.py:74
  182.9 0.1 mul.177
  183.1 0.1 copy.21
  183.2 0.1 reshape.75
  183.3 8.6 %all_to_all.29 = f32[8,1,1024]{2,1,0:T(1,128)S(1)} all-to-all(f32[8,1,1024]{2,1,0:T(1,128)S(1)} %reshape.75), channel_id=1, replica_groups=mesh['col_0'=4,'col_1'=16,'tm'=8] {'tm'}, dimensions={0} | all-to-all | bytes 65536 | tf_op jit(solution)/shard_map/all_to_all | solution.py:24
  191.9 0.5 broadcast.66
  192.4 0.7 reduce.2
  193.2 0.1 reshape.76
  193.3 0.1 bitcast_reduce_fusion
  193.4 0.4 copy.22
  193.9 10.4 %pmax.14 = f32[4]{0:T(128)S(1)} all-reduce(f32[4]{0:T(128)S(1)} %bitcast_reduce_fusion), channel_id=1, replica_groups=mesh['col_0'=4,'col_1'=16,'tm'=8] {'col_0'}, use_global_device_ids=true, to_apply=%region_5.6 | all-reduce | flops 4 | bytes 32 | tf_op jit(solution)/shard_map/pmax | solution.py:46
  204.3 1.4 broadcast_in_dim_reshape_reshape.4
  205.6 30.3 %pmax.15 = f32[4]{0:T(128)} all-reduce(f32[4]{0:T(128)S(1)} %pmax.14), channel_id=1, replica_groups=mesh['col_0'=4,'col_1'=16,'tm'=8] {'col_1'}, use_global_device_ids=true, to_apply=%region_6.7 | all-reduce | flops 4 | bytes 32 | tf_op jit(solution)/shard_map/pmax | solution.py:46
  (18 shorter events, 0.3 us)
Async XLA Ops:
  8.4 13.0 %all-to-all-start.1 = ((s32[8,4,75]{2,1,0:T(4,128)}), s32[8,4,75]{2,1,0:T(4,128)S(1)}, u32[]{:S(2)}, u32[]{:S(2)}) async-start(s32[8,4,75]{2,1,0:T(4,128)} %broadcast_in_dim.14), calls=%async_computation.1 | async-start | bytes 32768 | tf_op jit(solution)/shard_map/all_to_all | solution.py:24
  21.4 8.7 %all-to-all-start = ((f32[150,8,4]{0,2,1:T(4,128)}), f32[150,8,4]{0,2,1:T(4,128)S(1)}, u32[]{:S(2)}, u32[]{:S(2)}) async-start(f32[150,8,4]{0,2,1:T(4,128)} %all_to_all.20), calls=%async_computation | async-start | bytes 65536 | tf_op jit(solution)/shard_map/all_to_all | solution.py:89
  26.1 149.2 %all-gather.3.cloned.1.call-start = ((), (), s32[]{:S(2)}) async-start(), calls=%async_computation.3 | async-start | bytes 2785280 | tf_op jit(solution)/shard_map/all_gather | solution.py:34
  102.1 3.2 %copy-start = (bf16[1200,1536]{1,0:T(8,128)(2,1)S(1)}, bf16[1200,1536]{1,0:T(8,128)(2,1)}, u32[]{:S(2)}) copy-start(bf16[1200,1536]{1,0:T(8,128)(2,1)} %param.3) | copy-start | bytes 11059204
  175.3 3.0 %copy-start.1 = (bf16[1200,1536]{1,0:T(8,128)(2,1)S(1)}, bf16[1200,1536]{1,0:T(8,128)(2,1)}, u32[]{:S(2)}) copy-start(bf16[1200,1536]{1,0:T(8,128)(2,1)} %param.3) | copy-start | bytes 11059204
Sparse Core Ops, SparseCore 0:
  102.2 73.0 all-gather.2
where the time goes:
time: 243 us
  waiting for transfers between devices  75.2 us (31%)
  matrix products  63.3 us (26%)
  blocking collectives  62.4 us (26%)
  between operations  14.2 us (6%)
  starting transfers between devices  13.7 us (6%)
  local copies, waits for them, and re-layouts  9.04 us (4%)
  other arithmetic  4.89 us (2%)
    all_gather x1, waiting for transfers between devices, all_blocks(): parts = lax.all_gather(parts, axes[k], axis=0, tiled=True)  69 us
    pmax x2, blocking collectives, by_axis(): return functools.reduce(lax.pmax, axes, value)  40.8 us
    dot_general x1, matrix products, rotate_back(): jnp.einsum('sfv,tf->svt', rot_real, cos_back, precision=HIGHEST)  15.3 us
    dot_general x1, matrix products, rotate_back(): jnp.einsum('sfv,tf->svt', rot_imag, sin_back, precision=HIGHEST)  15.3 us
    dot_general x1, matrix products, body(): own_sin = jnp.dot(sin_every.T, own_frames, precision=HIGHEST)  14.1 us
    dot_general x1, matrix products, body(): own_cos = jnp.dot(cos_every.T, own_frames, precision=HIGHEST)  14 us
    all_gather x1, blocking collectives, all_blocks(): parts = lax.all_gather(parts, axes[k], axis=0, tiled=True)  13.1 us
    all_to_all x1, starting transfers between devices, sent_to_all(): return lax.all_to_all(copies, axis, split_axis=0, concat_axis=0, tiled=True)  9.04 us
  transfers between devices with their start and end apart: 3, of which 3 were waited for; matrix products, arithmetic and copies ran while one was open for 2% of the time, Pallas kernels for 0%

commit v1 on v0

--- a/solution.py
+++ b/solution.py
@@ -31,7 +31,9 @@
 def all_blocks(value, axes, sequence):
     parts = value[None]
     for k in sequence:
-        parts = lax.all_gather(parts, axes[k], axis=0, tiled=True)
+        parts = jnp.concatenate(
+            lax.all_to_all(jnp.stack([parts] * lax.axis_size(axes[k])), axes[k], 0, 0), axis=0
+        )
     current = [lax.axis_size(axes[k]) for k in reversed(sequence)]
     parts = parts.reshape(*current, *value.shape)
     turned = sorted(range(len(sequence)), key=lambda place: sequence[len(sequence) - 1 - place])

time: 243 us -> 281 us (1.16)
  the two profiles are of different devices: /device:TPU:8 before, /device:TPU:2 now
where the time goes in v1:
time: 281 us
  waiting for transfers between devices  118 us (42%)
  matrix products  63.5 us (23%)
  blocking collectives  60.6 us (22%)
  starting transfers between devices  20.6 us (7%)
  local copies, waits for them, and re-layouts  12.1 us (4%)
  other arithmetic  4.9 us (2%)
    all_to_all x1, waiting for transfers between devices, all_blocks(): lax.all_to_all(jnp.stack([parts] * lax.axis_size(axes[k])), axes[k], 0, 0)  109 us
    pmax x2, blocking collectives, by_axis(): return functools.reduce(lax.pmax, axes, value)  41.1 us
    dot_general x1, matrix products, rotate_back(): jnp.einsum('sfv,tf->svt', rot_real, cos_back, precision=HIGHEST)  15.5 us
    dot_general x1, matrix products, rotate_back(): jnp.einsum('sfv,tf->svt', rot_imag, sin_back, precision=HIGHEST)  15.3 us
    dot_general x1, matrix products, body(): own_sin = jnp.dot(sin_every.T, own_frames, precision=HIGHEST)  14.1 us
    dot_general x1, matrix products, body(): own_cos = jnp.dot(cos_every.T, own_frames, precision=HIGHEST)  14 us
    all_to_all x1, starting transfers between devices, all_blocks(): lax.all_to_all(jnp.stack([parts] * lax.axis_size(axes[k])), axes[k], 0, 0)  12.8 us
    all_to_all x1, blocking collectives, all_blocks(): lax.all_to_all(jnp.stack([parts] * lax.axis_size(axes[k])), axes[k], 0, 0)  11.7 us
  transfers between devices with their start and end apart: 3, of which 3 were waited for; matrix products, arithmetic and copies ran while one was open for 1% of the time, Pallas kernels for 0%

profile of v1, /device:TPU:2, one launch (start us, length us, event | category | flops | bytes accessed | tf_op | source)
XLA Modules:
  0.0 280.7 jit_solution(9408575678250956931)
XLA Ops:
  0.6 1.3 broadcast_in_dim.12
  1.9 4.5 %all-to-all-start.1 = ((s32[8,4,75]{2,1,0:T(4,128)}), s32[8,4,75]{2,1,0:T(4,128)S(1)}, u32[]{:S(2)}, u32[]{:S(2)}) async-start(s32[8,4,75]{2,1,0:T(4,128)} %broadcast_in_dim.12), calls=%async_computation.1 | async-start | bytes 32768 | tf_op jit(solution)/shard_map/all_to_all | solution.py:24
  6.4 1.4 all_to_all.26
  7.8 4.0 %all-to-all-done.1 = s32[8,4,75]{2,1,0:T(4,128)S(1)} async-done(((s32[8,4,75]{2,1,0:T(4,128)}), s32[8,4,75]{2,1,0:T(4,128)S(1)}, u32[]{:S(2)}, u32[]{:S(2)}) %all-to-all-start.1) | async-done | bytes 9632 | tf_op jit(solution)/shard_map/all_to_all | solution.py:24
  11.7 3.3 %all-to-all-start = ((f32[150,8,4]{0,2,1:T(4,128)}), f32[150,8,4]{0,2,1:T(4,128)S(1)}, u32[]{:S(2)}, u32[]{:S(2)}) async-start(f32[150,8,4]{0,2,1:T(4,128)} %all_to_all.26), calls=%async_computation | async-start | bytes 65536 | tf_op jit(solution)/shard_map/all_to_all | solution.py:91
  15.1 0.1 cosine_bitcast_fusion
  15.4 5.0 %all-to-all-done = f32[150,8,4]{0,2,1:T(4,128)S(1)} async-done(((f32[150,8,4]{0,2,1:T(4,128)}), f32[150,8,4]{0,2,1:T(4,128)S(1)}, u32[]{:S(2)}, u32[]{:S(2)}) %all-to-all-start) | async-done | bytes 19232 | tf_op jit(solution)/shard_map/all_to_all | solution.py:91
  20.5 0.1 all_to_all.29
  20.6 14.0 %fusion.19 = f32[600,4]{0,1:T(4,128)S(1)} fusion(f32[1200,4]{0,1:T(4,128)S(1)} %all_to_all.29, s32[600]{0:T(1024)S(1)} %iota_add_fusion), kind=kOutput, calls=%fused_computation.22 | convolution fusion | flops 41040000 | bytes 31200 | tf_op jit(solution)/shard_map/dot_general | solution.py:95
  34.6 14.1 %fusion.22 = f32[600,4]{0,1:T(4,128)S(1)} fusion(f32[1200,4]{0,1:T(4,128)S(1)} %all_to_all.29, s32[600]{0:T(1024)S(1)} %iota_add_fusion), kind=kOutput, calls=%fused_computation.23 | convolution fusion | flops 41040000 | bytes 31200 | tf_op jit(solution)/shard_map/dot_general | solution.py:96
  48.7 15.3 %fusion.10 = f32[4,4,1200]{2,1,0:T(4,128)S(1)} fusion(s32[600]{0:T(1024)S(1)} %iota_add_fusion, f32[600]{0:T(1024)S(1)} %select_multiply_fusion, f32[4,600]{1,0:T(4,128)S(1)} %sin.21, f32[600,4]{0,1:T(4,128)S(1)} %fusion.22, f32[4,600]{1,0:T(4,128)S(1)} %cos.21, f32[600,4]{0,1:T(4,128)S(1)} %fusion.19), kind=kOutput, calls=%fused_computation.13 | convolution fusion | flops 144758400 | bytes 120000 | tf_op jit(solution)/shard_map/sfv,tf->svt/dot_general | solution.py:64
  63.9 15.5 %multiply_reduce_fusion = (f32[4,4]{1,0:T(4,128)S(1)}, f32[4,4,1200]{2,1,0:T(4,128)S(1)}) fusion(f32[4,4,1200]{2,1,0:T(4,128)S(1)} %fusion.10, s32[600]{0:T(1024)S(1)} %iota_add_fusion, f32[600]{0:T(1024)S(1)} %select_multiply_fusion, f32[4,600]{1,0:T(4,128)S(1)} %sin.21, f32[600,4]{0,1:T(4,128)S(1)} %fusion.22, f32[4,600]{1,0:T(4,128)S(1)} %cos.21, ...), kind=kOutput, calls=%fused_computation.40 | convolution fusion | flops 144815984 | bytes 196864 | tf_op jit(solution)/shard_map/sfv,tf->svt/dot_general | solution.py:64
  79.6 11.7 %all_to_all.39 = bf16[4,1,4,4,1200]{4,2,3,1,0:T(4,128)(2,1)S(1)} all-to-all(bf16[4,1,4,4,1200]{4,2,3,1,0:T(4,128)(2,1)S(1)} %stack.6), channel_id=1, replica_groups=mesh['col_0'=4,'col_1'=16,'tm'=8] {'col_0'}, dimensions={0} | all-to-all | bytes 307200 | tf_op jit(solution)/shard_map/all_to_all | solution.py:35
  91.3 2.5 stack.7
  93.8 12.8 %all-to-all-start.3 = ((bf16[16,4,4,4,1200]{4,2,3,1,0:T(4,128)(2,1)}), bf16[16,4,4,4,1200]{4,2,3,1,0:T(4,128)(2,1)S(1)}, u32[]{:S(2)}, u32[]{:S(2)}) async-start(bf16[16,4,4,4,1200]{4,2,3,1,0:T(4,128)(2,1)} %stack.7), calls=%async_computation.3 | async-start | bytes 5242880 | tf_op jit(solution)/shard_map/all_to_all | solution.py:35
  106.6 2.8 convert_reduce_fusion
  109.4 0.4 copy-done
  109.8 1.0 fusion.2
  110.8 109.2 %all-to-all-done.3 = bf16[16,4,4,4,1200]{4,2,3,1,0:T(4,128)(2,1)S(1)} async-done(((bf16[16,4,4,4,1200]{4,2,3,1,0:T(4,128)(2,1)}), bf16[16,4,4,4,1200]{4,2,3,1,0:T(4,128)(2,1)S(1)}, u32[]{:S(2)}, u32[]{:S(2)}) %all-to-all-start.3) | async-done | bytes 2457632 | tf_op jit(solution)/shard_map/all_to_all | solution.py:35
  220.0 1.4 copy.20
  221.4 2.0 copy.21
  223.5 4.7 %abs_reduce_fusion = f32[4,256]{1,0:T(4,128)S(1)} fusion(bf16[1200,1536]{1,0:T(8,128)(2,1)S(1)} %copy-done.1, f32[1536]{0:T(1024)S(1)} %add_rsqrt_fusion, f32[1536]{0:T(1024)S(1)} %broadcast_multiply_fusion, bf16[4,256,1200]{2,0,1:T(4,128)(2,1)S(1)} %bitcast.43), kind=kOutput, calls=%fused_computation.6 | convolution fusion | flops 3785391104 | bytes 6160384 | tf_op jit(solution)/shard_map/srt,tc->src/dot_general | solution.py:76
  228.2 0.1 mul.177
  228.4 0.1 reshape.74
  228.5 7.8 %all_to_all.40 = f32[8,1,1024]{2,1,0:T(1,128)S(1)} all-to-all(f32[8,1,1024]{2,1,0:T(1,128)S(1)} %reshape.74), channel_id=1, replica_groups=mesh['col_0'=4,'col_1'=16,'tm'=8] {'tm'}, dimensions={0} | all-to-all | bytes 65536 | tf_op jit(solution)/shard_map/all_to_all | solution.py:24
  236.4 0.5 broadcast.69
  236.9 0.7 reduce.2
  237.7 0.1 bitcast_reduce_fusion
  237.8 0.4 copy.24
  238.3 10.6 %pmax.14 = f32[4]{0:T(128)S(1)} all-reduce(f32[4]{0:T(128)S(1)} %bitcast_reduce_fusion), channel_id=1, replica_groups=mesh['col_0'=4,'col_1'=16,'tm'=8] {'col_0'}, use_global_device_ids=true, to_apply=%region_5.6 | all-reduce | flops 4 | bytes 32 | tf_op jit(solution)/shard_map/pmax | solution.py:48
  248.9 1.4 broadcast_in_dim_reshape_reshape.4
  250.3 30.4 %pmax.15 = f32[4]{0:T(128)} all-reduce(f32[4]{0:T(128)S(1)} %pmax.14), channel_id=1, replica_groups=mesh['col_0'=4,'col_1'=16,'tm'=8] {'col_1'}, use_global_device_ids=true, to_apply=%region_6.7 | all-reduce | flops 4 | bytes 32 | tf_op jit(solution)/shard_map/pmax | solution.py:48
  (21 shorter events, 0.6 us)
Async XLA Ops:
  1.9 9.8 %all-to-all-start.1 = ((s32[8,4,75]{2,1,0:T(4,128)}), s32[8,4,75]{2,1,0:T(4,128)S(1)}, u32[]{:S(2)}, u32[]{:S(2)}) async-start(s32[8,4,75]{2,1,0:T(4,128)} %broadcast_in_dim.12), calls=%async_computation.1 | async-start | bytes 32768 | tf_op jit(solution)/shard_map/all_to_all | solution.py:24
  11.7 8.7 %all-to-all-start = ((f32[150,8,4]{0,2,1:T(4,128)}), f32[150,8,4]{0,2,1:T(4,128)S(1)}, u32[]{:S(2)}, u32[]{:S(2)}) async-start(f32[150,8,4]{0,2,1:T(4,128)} %all_to_all.26), calls=%async_computation | async-start | bytes 65536 | tf_op jit(solution)/shard_map/all_to_all | solution.py:91
  93.8 126.1 %all-to-all-start.3 = ((bf16[16,4,4,4,1200]{4,2,3,1,0:T(4,128)(2,1)}), bf16[16,4,4,4,1200]{4,2,3,1,0:T(4,128)(2,1)S(1)}, u32[]{:S(2)}, u32[]{:S(2)}) async-start(bf16[16,4,4,4,1200]{4,2,3,1,0:T(4,128)(2,1)} %stack.7), calls=%async_computation.3 | async-start | bytes 5242880 | tf_op jit(solution)/shard_map/all_to_all | solution.py:35
  106.6 3.2 %copy-start = (bf16[1200,1536]{1,0:T(8,128)(2,1)S(1)}, bf16[1200,1536]{1,0:T(8,128)(2,1)}, u32[]{:S(2)}) copy-start(bf16[1200,1536]{1,0:T(8,128)(2,1)} %param.3) | copy-start | bytes 11059204
  221.4 2.0 copy-start.1
